TPU v7x, 32 devices: a whole 2x2x4 slice. The times are simulated.
32 devices in a mesh: scan: 16 (over z, x, core), mode: 2 (over y).
Axes of the slice: x: 2, y: 2, z: 4, core: 2. Of those that a mesh axis runs over, the one named last changes fastest.
Arguments:
- object_field: float32 [2, 4096, 384], P(None, 'scan'), may hold values from -3 to 3, as said below
- eigen_probes: float32 [2, 2, 256, 256], P('mode'), may hold values from -2.1 to 2.1
- coeffs: float32 [64, 2, 2], P(('scan', 'mode')), may hold values from -4 to 4
- intensities: float32 [64, 256, 256], P(('scan', 'mode')), may hold values from 0.05 to 1
- positions: int32 [64, 2], P(('scan', 'mode')), may hold values from 0 to 3840, as said below
Outputs:
- object_new: float32 [2, 4096, 384], P(None, 'scan')
- probes_new: float32 [2, 2, 256, 256], P('mode')
- coeffs_new: float32 [64, 2, 2], P(('scan', 'mode'))
Inputs may be any that keep to these rules, and one draw needn't show every extreme that they name: Pattern j belongs to tile t = j // 4: t * 256 <= positions[j,0] < t * 256 + 256, and positions[j,0] <= 3840; in every tile but the last some pattern has positions[j,0] = t * 256 + 255. positions[j,1] <= 128, reached in every tile. `object_field`: each pixel's magnitude lies between 0.3 and 3.
All inputs are finite; a program needn't handle non-finite values.
Results may differ from a plain program's by a relative error of at most 0.0003.
Values sent between devices are 32-bit elements; how exact they have to be, the bound alone decides.
A program may use at most 128 MiB of HBM per device.

v0:
```python
import functools
import math

import jax
import jax.numpy as jnp
import ml_dtypes
import numpy as np
from jax import lax
from jax.experimental import pallas as pl
from jax.experimental.pallas import tpu as pltpu
from jax.sharding import PartitionSpec as P

MAGNITUDE_FLOOR = 0.5
OBJECT_REGULARIZER = 1.0
EPSILON = 1e-05
MESH = pl.DeviceIdType.MESH
BLOCK = 32
EXTRA = 8
VMEM_BYTES = 56 * 1024 * 1024


def dft_tables(length):
    indices = np.arange(length)
    angle = (indices[:, None] * indices[None, :] % length) * (2.0 * math.pi / length)
    cosine = np.cos(angle) / math.sqrt(length)
    sine = -np.sin(angle) / math.sqrt(length)
    right = np.block([[cosine, sine], [-sine, cosine]])
    left = np.block([[cosine, -sine], [sine, cosine]])
    found = []
    for table in (right, left):
        high = table.astype(ml_dtypes.bfloat16)
        low = (table - high.astype(np.float64)).astype(ml_dtypes.bfloat16)
        found += [high, low]
    return found


def radices(count):
    rest = count // 2
    first = 1
    while first * first * 4 <= rest:
        first *= 2
    return first, rest // first


def gather_kernel(scans, modes, probe_ref, object_ref, gathered_ref, next_ref, *sems):
    send_y, recv_y, send_c, recv_c, send_o, recv_o = sems
    s = lax.axis_index("scan")
    m = lax.axis_index("mode")
    half = probe_ref.shape[0] // 2
    core = lax.rem(s, 2)
    sibling = s + 1 - 2 * core
    rows = pl.ds(pl.multiple_of(core * half, half), half)
    barrier = pltpu.get_barrier_semaphore()
    pl.semaphore_signal(barrier, inc=1, device_id=(sibling, m), device_id_type=MESH)
    for step in range(1, modes):
        other = lax.rem(m + step, modes)
        pl.semaphore_signal(barrier, inc=1, device_id=(s, other), device_id_type=MESH)

    @pl.when(s > 0)
    def _():
        pl.semaphore_signal(barrier, inc=1, device_id=(s - 1, m), device_id_type=MESH)

    @pl.when(s < scans - 1)
    def _():
        pl.semaphore_signal(barrier, inc=1, device_id=(s + 1, m), device_id_type=MESH)

    inner = jnp.minimum(s, 1) + jnp.minimum(scans - 1 - s, 1)
    pl.semaphore_wait(barrier, modes + inner)

    def object_copy(target):
        return pltpu.make_async_remote_copy(
            src_ref=object_ref, dst_ref=next_ref, send_sem=send_o, recv_sem=recv_o,
            device_id=(target, m), device_id_type=MESH)

    def mode_copy(step):
        return pltpu.make_async_remote_copy(
            src_ref=probe_ref.at[rows], dst_ref=gathered_ref.at[m, rows],
            send_sem=send_y.at[step - 1], recv_sem=recv_y.at[step - 1],
            device_id=(s, lax.rem(m + step, modes)), device_id_type=MESH)

    def sibling_copy(step):
        source = lax.rem(m + modes - step, modes)
        return pltpu.make_async_remote_copy(
            src_ref=gathered_ref.at[source, rows], dst_ref=gathered_ref.at[source, rows],
            send_sem=send_c.at[step - 1], recv_sem=recv_c.at[step - 1],
            device_id=(sibling, m), device_id_type=MESH)

    for step in range(1, modes):
        mode_copy(step).start()

    @pl.when(s > 0)
    def _():
        object_copy(s - 1).start()

    gathered_ref[m] = probe_ref[...]
    for step in range(1, modes):
        mode_copy(step).wait_recv()
        sibling_copy(step).start()
    for step in range(1, modes):
        mode_copy(step).wait_send()
        sibling_copy(step).wait_send()
        sibling_copy(step).wait_recv()

    @pl.when(s > 0)
    def _():
        object_copy(s - 1).wait_send()

    @pl.when(s < scans - 1)
    def _():
        object_copy(s + 1).wait_recv()


def compute_kernel(modes, place_ref, coef_ref, probe_ref, own_ref, next_ref, inten_ref,
                   rh_ref, rl_ref, lh_ref, ll_ref, terms_ref, grad_ref, coef_out_ref,
                   ext_ref, wave_ref, window_ref, mixed_ref, flat_ref, tall_ref, out_ref,
                   inner_ref, weight_ref, norm_ref):
    count, length = inten_ref.shape[0], inten_ref.shape[1]
    columns = own_ref.shape[2]
    blocks = length // BLOCK
    ext_ref[:, :length] = own_ref[...]
    ext_ref[:, length:] = next_ref[...]
    terms_ref[...] = jnp.zeros_like(terms_ref)
    grad_ref[...] = jnp.zeros_like(grad_ref)

    def folded(value):
        return jnp.sum(value.reshape(BLOCK // 8, 8, length), axis=0)

    def split(value):
        high = value.astype(jnp.bfloat16)
        return high, (value - high.astype(jnp.float32)).astype(jnp.bfloat16)

    def put_flat(rows, real, imag):
        for slot, value in enumerate((real, imag)):
            high, low = split(value)
            flat_ref[rows, slot * length:(slot + 1) * length] = high
            flat_ref[rows, (2 + slot) * length:(3 + slot) * length] = low

    def dot(a, b):
        return jnp.dot(a, b, preferred_element_type=jnp.float32)

    def right_apply(high_ref, low_ref):
        high = flat_ref[:, :2 * length]
        low = flat_ref[:, 2 * length:]
        result = dot(high, high_ref[...]) + dot(low, high_ref[...]) + dot(high, low_ref[...])
        for slot in range(2):
            part_high, part_low = split(result[:, slot * length:(slot + 1) * length])
            tall_ref[slot * length:(slot + 1) * length] = part_high
            tall_ref[(2 + slot) * length:(3 + slot) * length] = part_low

    def left_apply(high_ref, low_ref):
        high = tall_ref[:2 * length]
        low = tall_ref[2 * length:]
        out_ref[...] = dot(high_ref[...], high) + dot(high_ref[...], low) + dot(low_ref[...], high)

    norm_ref[...] = jnp.zeros_like(norm_ref)

    def norms(index, carry):
        for mode in range(modes):
            rows = pl.ds(pl.multiple_of(index * BLOCK, BLOCK), BLOCK)
            value = probe_ref[mode, rows]
            norm_ref[mode] += folded(value * value)
        return carry

    lax.fori_loop(0, 2 * blocks, norms, 0)

    def pattern(b, carry):
        top = place_ref[b, 0]
        left = place_ref[b, 1]
        back_shift = lax.rem(columns - left, columns)
        within = lax.rem(top, 8)
        top_tile = top - within
        up_shift = lax.rem(8 - within, 8)
        sublane = lax.broadcasted_iota(jnp.int32, (BLOCK // 8, 8, length), 1)
        wide = lax.broadcasted_iota(jnp.int32, (BLOCK // 8 + 1, 8, columns), 1)
        inner_ref[...] = jnp.zeros_like(inner_ref)
        weight_ref[...] = jnp.zeros_like(weight_ref)

        def first(index, carry):
            base = pl.multiple_of(index * BLOCK, BLOCK)
            rows = pl.ds(base, BLOCK)
            lower = pl.ds(pl.multiple_of(base + length, BLOCK), BLOCK)
            pr = jnp.zeros((BLOCK, length), jnp.float32)
            pi = jnp.zeros((BLOCK, length), jnp.float32)
            for mode in range(modes):
                cr, ci = coef_ref[b, 0, mode], coef_ref[b, 1, mode]
                ur, ui = probe_ref[mode, rows], probe_ref[mode, lower]
                pr = pr + cr * ur - ci * ui
                pi = pi + cr * ui + ci * ur
            window = []
            for part in range(2):
                strip = ext_ref[part, pl.ds(pl.multiple_of(top_tile + base, 8), BLOCK + 8), :]
                strip = pltpu.roll(strip, back_shift, 1)[:, :length]
                turned = pltpu.roll(strip.reshape(BLOCK // 8 + 1, 8, length), up_shift, 1)
                kept = jnp.where(sublane < 8 - within, turned[:-1], turned[1:])
                window.append(kept.reshape(BLOCK, length))
            wr, wi = window
            window_ref[rows], window_ref[lower] = wr, wi
            mixed_ref[rows], mixed_ref[lower] = pr, pi
            weight_ref[...] += folded(wr * wr + wi * wi)
            real = pr * wr - pi * wi
            imag = pr * wi + pi * wr
            wave_ref[rows], wave_ref[lower] = real, imag
            put_flat(rows, real, imag)
            return carry

        lax.fori_loop(0, blocks, first, 0)
        right_apply(rh_ref, rl_ref)
        left_apply(lh_ref, ll_ref)

        def second(index, carry):
            base = pl.multiple_of(index * BLOCK, BLOCK)
            rows = pl.ds(base, BLOCK)
            lower = pl.ds(pl.multiple_of(base + length, BLOCK), BLOCK)
            real, imag = out_ref[rows], out_ref[lower]
            power = jnp.maximum(real * real + imag * imag, MAGNITUDE_FLOOR * MAGNITUDE_FLOOR)
            factor = jnp.sqrt(inten_ref[b, rows] / power)
            put_flat(rows, real * factor, imag * factor)
            return carry

        lax.fori_loop(0, blocks, second, 0)
        right_apply(lh_ref, ll_ref)
        left_apply(rh_ref, rl_ref)

        def third(index, carry):
            base = pl.multiple_of(index * BLOCK, BLOCK)
            rows = pl.ds(base, BLOCK)
            lower = pl.ds(pl.multiple_of(base + length, BLOCK), BLOCK)
            dr = out_ref[rows] - wave_ref[rows]
            di = out_ref[lower] - wave_ref[lower]
            pr, pi = mixed_ref[rows], mixed_ref[lower]
            wr, wi = window_ref[rows], window_ref[lower]
            pieces = (pr * dr + pi * di, pr * di - pi * dr, pr * pr + pi * pi)
            for part, piece in enumerate(pieces):
                padded = jnp.concatenate(
                    [piece, jnp.zeros((BLOCK, columns - length), jnp.float32)], axis=1)
                padded = pltpu.roll(padded, left, 1).reshape(BLOCK // 8, 8, columns)
                padded = pltpu.roll(padded, within, 1)
                edge = jnp.zeros((1, 8, columns), jnp.float32)
                placed = jnp.where(
                    wide >= within,
                    jnp.concatenate([padded, edge], axis=0),
                    jnp.concatenate([edge, padded], axis=0))
                spot = pl.ds(pl.multiple_of(top_tile + base, 8), BLOCK + 8)
                terms_ref[part, spot, :] += placed.reshape(BLOCK + 8, columns)
            gr = wr * dr + wi * di
            gi = wr * di - wi * dr
            for mode in range(modes):
                cr, ci = coef_ref[b, 0, mode], coef_ref[b, 1, mode]
                ur, ui = probe_ref[mode, rows], probe_ref[mode, lower]
                grad_ref[0, mode, rows] += cr * gr + ci * gi
                grad_ref[1, mode, rows] += cr * gi - ci * gr
                inner_ref[mode, 0] += folded(ur * gr + ui * gi)
                inner_ref[mode, 1] += folded(ur * gi - ui * gr)
            return carry

        lax.fori_loop(0, blocks, third, 0)

        def total(value):
            return jnp.sum(jnp.sum(value, axis=1, keepdims=True), axis=0, keepdims=True)

        weight = total(weight_ref[...]) * (1.0 / (length * length))
        lanes = lax.broadcasted_iota(jnp.int32, (1, modes), 1)
        found = [jnp.zeros((1, modes), jnp.float32)] * 2
        for mode in range(modes):
            cr, ci = coef_ref[b, 0, mode], coef_ref[b, 1, mode]
            denominator = total(norm_ref[mode]) * weight + EPSILON
            for part, c in enumerate((cr, ci)):
                value = c + total(inner_ref[mode, part]) / denominator
                found[part] = jnp.where(lanes == mode, value, found[part])
            share = jnp.broadcast_to((cr * cr + ci * ci) * weight, (1, length))
            for part in range(2):
                grad_ref[part, mode, length:] += jnp.broadcast_to(share, (EXTRA, length))
        coef_out_ref[b] = jnp.concatenate(found, axis=0)
        return carry

    lax.fori_loop(0, count, pattern, 0)


def reduce_kernel(scans, modes, terms_ref, grad_ref, object_ref, probe_ref,
                  object_out_ref, probe_out_ref,
                  core_in, mode_in, stage1, in1, stage2, in2, shift_in, stage_n, numer_in,
                  send_g, recv_g, send_1, recv_1, send_2, recv_2, send_b, recv_b,
                  send_s, recv_s, send_n, recv_n, send_a, recv_a):
    s = lax.axis_index("scan")
    m = lax.axis_index("mode")
    r1, r2 = radices(scans)
    length = object_ref.shape[1]
    d0 = lax.rem(s, 2)
    d1 = lax.rem(s // 2, r1)
    d2 = s // (2 * r1)
    b1, b2 = length // r1, length // (r1 * r2)
    rows_m = length // modes
    sibling = (s + 1 - 2 * d0, m)

    def peer1(step):
        return ((d2 * r1 + lax.rem(d1 + step, r1)) * 2 + d0, m)

    def peer2(step):
        return ((lax.rem(d2 + step, r2) * r1 + d1) * 2 + d0, m)

    def peer_m(step):
        return (s, lax.rem(m + step, modes))

    peers = [sibling] + [peer1(i) for i in range(1, r1)] + [peer2(i) for i in range(1, r2)]
    peers += [peer_m(i) for i in range(1, modes)]
    barrier = pltpu.get_barrier_semaphore()
    for peer in peers:
        pl.semaphore_signal(barrier, inc=1, device_id=peer, device_id_type=MESH)

    @pl.when(s > 0)
    def _():
        pl.semaphore_signal(barrier, inc=1, device_id=(s - 1, m), device_id_type=MESH)

    @pl.when(s < scans - 1)
    def _():
        pl.semaphore_signal(barrier, inc=1, device_id=(s + 1, m), device_id_type=MESH)

    inner = jnp.minimum(s, 1) + jnp.minimum(scans - 1 - s, 1)
    pl.semaphore_wait(barrier, len(peers) + inner)

    def remote(src, dst, send, recv, peer):
        return pltpu.make_async_remote_copy(
            src_ref=src, dst_ref=dst, send_sem=send, recv_sem=recv,
            device_id=peer, device_id_type=MESH)

    def chunk(owner):
        return pl.ds(pl.multiple_of(owner * rows_m, rows_m), rows_m)

    def shift_copy(step, target):
        owner = lax.rem(m + step, modes)
        away = pl.ds(pl.multiple_of(length + owner * rows_m, rows_m), rows_m)
        return remote(terms_ref.at[:, away], shift_in.at[:, chunk(owner)],
                      send_s.at[step - 1], recv_s.at[step - 1], (target, m))

    sends = []
    core_copy = remote(grad_ref.at[1 - d0], core_in, send_g.at[0], recv_g.at[0], sibling)
    core_copy.start()
    sends.append(core_copy)

    @pl.when(s < scans - 1)
    def _():
        for step in range(1, modes + 1):
            shift_copy(step, s + 1).start()

    @pl.when(s == 0)
    def _():
        shift_in[...] = jnp.zeros_like(shift_in)

    def shift_wait(step):
        @pl.when(s > 0)
        def _():
            shift_copy(step, s - 1).wait_recv()

    core_copy.wait_recv()
    mode_copies = []
    for step in range(1, modes):
        owner = lax.rem(m + step, modes)
        core_in[owner] = core_in[owner] + grad_ref[d0, owner]
        copy = remote(core_in.at[owner], mode_in.at[step - 1],
                      send_g.at[step], recv_g.at[step], peer_m(step))
        copy.start()
        mode_copies.append(copy)
    numer_copies = []
    for step in range(1, modes):
        owner = lax.rem(m + step, modes)
        shift_wait(step)
        stage_n[step - 1] = terms_ref[:, chunk(owner)] + shift_in[:, chunk(owner)]
        copy = remote(stage_n.at[step - 1], numer_in.at[step - 1],
                      send_n.at[step - 1], recv_n.at[step - 1], peer_m(step))
        copy.start()
        numer_copies.append(copy)
    total = core_in[m] + grad_ref[d0, m]
    for step in range(1, modes):
        mode_copies[step - 1].wait_recv()
        total = total + mode_in[step - 1]
    for index in range(r1):
        stage1[index, :b1] = total[index * b1:(index + 1) * b1]
        stage1[index, b1:] = total[length:]
    copies1 = []
    for step in range(1, r1):
        copy = remote(stage1.at[lax.rem(d1 + step, r1)], in1.at[step - 1],
                      send_1.at[step - 1], recv_1.at[step - 1], peer1(step))
        copy.start()
        copies1.append(copy)
    total = stage1[d1]
    for step in range(1, r1):
        copies1[step - 1].wait_recv()
        total = total + in1[step - 1]
    for index in range(r2):
        stage2[index, :b2] = total[index * b2:(index + 1) * b2]
        stage2[index, b2:] = total[b1:]
    copies2 = []
    for step in range(1, r2):
        copy = remote(stage2.at[lax.rem(d2 + step, r2)], in2.at[step - 1],
                      send_2.at[step - 1], recv_2.at[step - 1], peer2(step))
        copy.start()
        copies2.append(copy)
    total = stage2[d2]
    for step in range(1, r2):
        copies2[step - 1].wait_recv()
        total = total + in2[step - 1]
    block0 = pl.ds(pl.multiple_of(d0 * length, length), length)
    start1 = d0 * length + d1 * b1
    block1 = pl.ds(pl.multiple_of(start1, b1), b1)
    block2 = pl.ds(pl.multiple_of(start1 + d2 * b2, b2), b2)
    probe_out_ref[block2] = probe_ref[block2] + total[:b2] / total[b2:b2 + 1]
    back2 = []
    for step in range(1, r2):
        copy = remote(probe_out_ref.at[block2], probe_out_ref.at[block2],
                      send_b.at[step - 1], recv_b.at[step - 1], peer2(step))
        copy.start()
        back2.append(copy)
    shift_wait(modes)
    for step in range(1, modes):
        numer_copies[step - 1].wait_recv()
    mine = chunk(m)

    def owned(part):
        value = terms_ref[part, mine] + shift_in[part, mine]
        for step in range(1, modes):
            value = value + numer_in[step - 1, part]
        return value

    scale = owned(2) + OBJECT_REGULARIZER
    for part in range(2):
        object_out_ref[part, mine] = object_ref[part, mine] + owned(part) / scale
    object_copies = []
    for step in range(1, modes):
        copy = remote(object_out_ref.at[:, mine], object_out_ref.at[:, mine],
                      send_a.at[step - 1], recv_a.at[step - 1], peer_m(step))
        copy.start()
        object_copies.append(copy)
    for copy in back2:
        copy.wait_recv()
    back1 = []
    for step in range(1, r1):
        slot = r2 - 1 + step - 1
        copy = remote(probe_out_ref.at[block1], probe_out_ref.at[block1],
                      send_b.at[slot], recv_b.at[slot], peer1(step))
        copy.start()
        back1.append(copy)
    for copy in back1:
        copy.wait_recv()
    slot = r2 + r1 - 2
    back0 = remote(probe_out_ref.at[block0], probe_out_ref.at[block0],
                   send_b.at[slot], recv_b.at[slot], sibling)
    back0.start()
    back0.wait_recv()
    for copy in object_copies:
        copy.wait_recv()

    @pl.when(s < scans - 1)
    def _():
        for step in range(1, modes + 1):
            shift_copy(step, s + 1).wait_send()

    for copy in sends + mode_copies + numer_copies + copies1 + copies2 + back2 + back1:
        copy.wait_send()
    for copy in object_copies + [back0]:
        copy.wait_send()


def on_device(scans, modes, object_field, eigen_probes, coeffs, intensities, positions):
    length = eigen_probes.shape[2]
    columns = object_field.shape[2]
    f32 = jnp.float32
    vmem = pl.BlockSpec(memory_space=pltpu.VMEM)
    smem = pl.BlockSpec(memory_space=pltpu.SMEM)
    dma = pltpu.SemaphoreType.DMA
    probe = eigen_probes.reshape(2 * length, length)
    others = max(modes - 1, 1)
    r1, r2 = radices(scans)
    b1, b2 = length // r1, length // (r1 * r2)
    gathered, following = pl.pallas_call(
        functools.partial(gather_kernel, scans, modes),
        out_shape=(
            jax.ShapeDtypeStruct((modes, 2 * length, length), f32),
            jax.ShapeDtypeStruct(object_field.shape, f32),
        ),
        in_specs=[vmem] * 2,
        out_specs=(vmem, vmem),
        scratch_shapes=[dma((others,))] * 4 + [dma, dma],
        compiler_params=pltpu.CompilerParams(
            collective_id=0, has_side_effects=True, vmem_limit_bytes=VMEM_BYTES),
        name="gather_probes",
    )(probe, object_field)
    row_start = positions[:, 0] - lax.axis_index("scan") * length
    place = jnp.stack([row_start, positions[:, 1]], axis=1)
    tables = [jnp.asarray(table) for table in dft_tables(length)]
    terms, grads, coeffs_new = pl.pallas_call(
        functools.partial(compute_kernel, modes),
        out_shape=(
            jax.ShapeDtypeStruct((3, 2 * length, columns), f32),
            jax.ShapeDtypeStruct((2, modes, length + EXTRA, length), f32),
            jax.ShapeDtypeStruct(coeffs.shape, f32),
        ),
        in_specs=[smem, smem] + [vmem] * 8,
        out_specs=(vmem, vmem, vmem),
        scratch_shapes=[
            pltpu.VMEM((2, 2 * length, columns), f32),
            pltpu.VMEM((2 * length, length), f32),
            pltpu.VMEM((2 * length, length), f32),
            pltpu.VMEM((2 * length, length), f32),
            pltpu.VMEM((length, 4 * length), jnp.bfloat16),
            pltpu.VMEM((4 * length, length), jnp.bfloat16),
            pltpu.VMEM((2 * length, length), f32),
            pltpu.VMEM((modes, 2, 8, length), f32),
            pltpu.VMEM((8, length), f32),
            pltpu.VMEM((modes, 8, length), f32),
        ],
        compiler_params=pltpu.CompilerParams(vmem_limit_bytes=VMEM_BYTES),
        name="local_terms",
    )(place, coeffs, gathered, object_field, following, intensities, *tables)
    rows_m = length // modes
    object_new, probes_new = pl.pallas_call(
        functools.partial(reduce_kernel, scans, modes),
        out_shape=(
            jax.ShapeDtypeStruct(object_field.shape, f32),
            jax.ShapeDtypeStruct((2 * length, length), f32),
        ),
        in_specs=[vmem] * 4,
        out_specs=(vmem, vmem),
        scratch_shapes=[
            pltpu.VMEM((modes, length + EXTRA, length), f32),
            pltpu.VMEM((others, length + EXTRA, length), f32),
            pltpu.VMEM((r1, b1 + EXTRA, length), f32),
            pltpu.VMEM((max(r1 - 1, 1), b1 + EXTRA, length), f32),
            pltpu.VMEM((r2, b2 + EXTRA, length), f32),
            pltpu.VMEM((max(r2 - 1, 1), b2 + EXTRA, length), f32),
            pltpu.VMEM((3, length, columns), f32),
            pltpu.VMEM((others, 3, rows_m, columns), f32),
            pltpu.VMEM((others, 3, rows_m, columns), f32),
            dma((modes,)), dma((modes,)),
            dma((max(r1 - 1, 1),)), dma((max(r1 - 1, 1),)),
            dma((max(r2 - 1, 1),)), dma((max(r2 - 1, 1),)),
            dma((r1 + r2 - 1,)), dma((r1 + r2 - 1,)),
            dma((modes,)), dma((modes,)),
            dma((others,)), dma((others,)),
            dma((others,)), dma((others,)),
        ],
        compiler_params=pltpu.CompilerParams(
            collective_id=1, has_side_effects=True, vmem_limit_bytes=VMEM_BYTES),
        name="reduce_terms",
    )(terms, grads, object_field, probe)
    return object_new, probes_new.reshape(eigen_probes.shape), coeffs_new


def solution(mesh):
    return jax.shard_map(
        functools.partial(on_device, mesh.shape["scan"], mesh.shape["mode"]),
        mesh=mesh,
        in_specs=(
            P(None, "scan", None),
            P("mode", None, None, None),
            P(("scan", "mode"), None, None),
            P(("scan", "mode"), None, None),
            P(("scan", "mode"), None),
        ),
        out_specs=(
            P(None, "scan", None),
            P("mode", None, None, None),
            P(("scan", "mode"), None, None),
        ),
        check_vma=False,
    )
```

profile of v0, /device:TPU:0, one launch (start us, length us, event | category | flops | bytes accessed | tf_op | source)
XLA Modules:
  0.0 77.1 jit_solution(13163283222607849748)
XLA Ops:
  0.6 0.8 %slice_subtract_fusion = (s32[2,1]{1,0:T(2,128)S(1)}, s32[2,1]{1,0:T(2,128)S(1)}) fusion(s32[2,2]{1,0:T(2,128)} %param.13, s32[]{:T(128)S(6)} %mul.3), kind=kLoop, calls=%fused_computation.1 | loop fusion | flops 2 | bytes 36 | tf_op jit(solution)/shard_map/sub | solution.py:487
  1.5 0.6 pad_add_fusion.place_ref
  2.1 13.6 %gather_probes.1 = (f32[2,512,256]{2,1,0:T(8,128)}, f32[2,256,384]{2,1,0:T(8,128)}) custom-call(f32[512,256]{1,0:T(8,128)} %bitcast.2, f32[2,256,384]{2,1,0:T(8,128)} %object_ref.3), custom_call_target="tpu_custom_call" | custom-call | tf_op jit(solution)/shard_map/gather_probes/pallas_call | solution.py:474
  15.7 15.7 %local_terms.1 = (f32[3,512,384]{2,1,0:T(8,128)}, f32[2,2,264,256]{3,2,1,0:T(8,128)}, f32[2,2,2]{2,1,0:T(2,128)}) custom-call(s32[2,2]{1,0:T(2,128)} %pad_add_fusion.place_ref, f32[2,2,2]{2,1,0:T(2,128)} %coef_ref.1, f32[2,512,256]{2,1,0:T(8,128)} %get-tuple-element.10.probe_ref, f32[2,256,384]{2,1,0:T(8,128)} %object_ref.3, ...), custom_call_target="tpu_custom_call" | custom-call | tf_op jit(solution)/shard_map/local_terms/pallas_call | solution.py:490
  31.3 41.8 %reduce_terms.1 = (f32[2,256,384]{2,1,0:T(8,128)}, f32[512,256]{1,0:T(8,128)}) custom-call(f32[3,512,384]{2,1,0:T(8,128)} %get-tuple-element.12.terms_ref, f32[2,2,264,256]{3,2,1,0:T(8,128)} %get-tuple-element.13.grad_ref, f32[2,256,384]{2,1,0:T(8,128)} %object_ref.3, f32[512,256]{1,0:T(8,128)} %bitcast.3), custom_call_target="tpu_custom_call" | custom-call | tf_op jit(solution)/shard_map/reduce_terms/pallas_call | solution.py:515
  73.2 2.1 %copy.14 = f32[2,256,384]{2,1,0:T(8,128)} copy(f32[2,256,384]{2,1,0:T(8,128)} %get-tuple-element.22) | data formatting | bytes 1572864
  75.2 1.9 %copy.15 = f32[1,2,256,256]{3,2,1,0:T(8,128)} copy(f32[1,2,256,256]{3,2,1,0:T(8,128)} %bitcast.4) | data formatting | bytes 1048576
where the time goes:
time: 77.3 us; the launch traced here: 77.1 us
  Pallas kernels  71 us (92%)
  local copies, waits for them, and re-layouts  3.93 us (5%)
  other arithmetic  1.46 us (2%)
    pallas_call x1, Pallas kernels, on_device(): pl.pallas_call(functools.partial(reduce_kernel, scans, modes), out_shape=...  41.8 us
    pallas_call x1, Pallas kernels, on_device(): pl.pallas_call(functools.partial(compute_kernel, modes), out_shape=(jax.S...  15.7 us
    pallas_call x1, Pallas kernels, on_device(): pl.pallas_call(functools.partial(gather_kernel, scans, modes), out_shape=...  13.6 us
    unnamed x2, local copies, waits for them, and re-layouts  3.93 us

commit v1 on v0

--- a/solution.py
+++ b/solution.py
@@ -42,8 +42,10 @@
     return first, rest // first
 
 
-def gather_kernel(scans, modes, probe_ref, object_ref, gathered_ref, next_ref, *sems):
-    send_y, recv_y, send_c, recv_c, send_o, recv_o = sems
+def gather_kernel(scans, modes, probe_ref, object_ref, inten_ref, place_ref, coef_ref,
+                  gathered_ref, next_ref, inten_out_ref, place_out_ref, coef_out_ref,
+                  send_y, recv_y, send_c, recv_c, send_o, recv_o, send_t, recv_t):
+    count = inten_ref.shape[0]
     s = lax.axis_index("scan")
     m = lax.axis_index("mode")
     half = probe_ref.shape[0] // 2
@@ -85,6 +87,17 @@
             send_sem=send_c.at[step - 1], recv_sem=recv_c.at[step - 1],
             device_id=(sibling, m), device_id_type=MESH)
 
+    held = pl.ds(m * count, count)
+    tile_pairs = ((place_ref, place_out_ref.at[m]), (coef_ref, coef_out_ref.at[m]),
+                  (inten_ref, inten_out_ref.at[held]))
+
+    def tile_copies(step):
+        return [pltpu.make_async_remote_copy(
+            src_ref=src, dst_ref=dst,
+            send_sem=send_t.at[step - 1, slot], recv_sem=recv_t.at[step - 1, slot],
+            device_id=(s, lax.rem(m + step, modes)), device_id_type=MESH)
+            for slot, (src, dst) in enumerate(tile_pairs)]
+
     for step in range(1, modes):
         mode_copy(step).start()
 
@@ -92,7 +105,14 @@
     def _():
         object_copy(s - 1).start()
 
+    for step in range(1, modes):
+        for copy in tile_copies(step):
+            copy.start()
+
     gathered_ref[m] = probe_ref[...]
+    place_out_ref[m] = place_ref[...]
+    coef_out_ref[m] = coef_ref[...]
+    inten_out_ref[held] = inten_ref[...]
     for step in range(1, modes):
         mode_copy(step).wait_recv()
         sibling_copy(step).start()
@@ -100,6 +120,8 @@
         mode_copy(step).wait_send()
         sibling_copy(step).wait_send()
         sibling_copy(step).wait_recv()
+        for copy in tile_copies(step):
+            copy.wait()
 
     @pl.when(s > 0)
     def _():
@@ -114,7 +136,10 @@
                    rh_ref, rl_ref, lh_ref, ll_ref, terms_ref, grad_ref, coef_out_ref,
                    ext_ref, wave_ref, window_ref, mixed_ref, flat_ref, tall_ref, out_ref,
                    inner_ref, weight_ref, norm_ref):
-    count, length = inten_ref.shape[0], inten_ref.shape[1]
+    patterns, length = inten_ref.shape[0], inten_ref.shape[1]
+    count = patterns // modes
+    me = lax.axis_index("mode")
+    tile_top = lax.axis_index("scan") * length
     columns = own_ref.shape[2]
     blocks = length // BLOCK
     ext_ref[:, :length] = own_ref[...]
@@ -139,18 +164,20 @@
         return jnp.dot(a, b, preferred_element_type=jnp.float32)
 
     def right_apply(high_ref, low_ref):
-        high = flat_ref[:, :2 * length]
-        low = flat_ref[:, 2 * length:]
-        result = dot(high, high_ref[...]) + dot(low, high_ref[...]) + dot(high, low_ref[...])
+        field = flat_ref[...]
+        table = high_ref[...]
+        result = dot(jnp.concatenate([field, field[:, :2 * length]], axis=1),
+                     jnp.concatenate([table, table, low_ref[...]], axis=0))
         for slot in range(2):
             part_high, part_low = split(result[:, slot * length:(slot + 1) * length])
             tall_ref[slot * length:(slot + 1) * length] = part_high
             tall_ref[(2 + slot) * length:(3 + slot) * length] = part_low
 
     def left_apply(high_ref, low_ref):
-        high = tall_ref[:2 * length]
-        low = tall_ref[2 * length:]
-        out_ref[...] = dot(high_ref[...], high) + dot(high_ref[...], low) + dot(low_ref[...], high)
+        field = tall_ref[...]
+        table = high_ref[...]
+        out_ref[...] = dot(jnp.concatenate([table, table, low_ref[...]], axis=1),
+                           jnp.concatenate([field, field[:2 * length]], axis=0))
 
     norm_ref[...] = jnp.zeros_like(norm_ref)
 
@@ -163,9 +190,16 @@
 
     lax.fori_loop(0, 2 * blocks, norms, 0)
 
-    def pattern(b, carry):
-        top = place_ref[b, 0]
-        left = place_ref[b, 1]
+    def pattern(own, index, carry):
+        b = lax.rem(index, count)
+        owner = lax.rem(me + index // count, modes)
+        b_all = owner * count + b
+
+        def coef(mode):
+            return coef_ref[owner, b, mode], coef_ref[owner, b, modes + mode]
+
+        top = place_ref[owner, b, 0] - tile_top
+        left = place_ref[owner, b, 1]
         back_shift = lax.rem(columns - left, columns)
         within = lax.rem(top, 8)
         top_tile = top - within
@@ -182,7 +216,7 @@
             pr = jnp.zeros((BLOCK, length), jnp.float32)
             pi = jnp.zeros((BLOCK, length), jnp.float32)
             for mode in range(modes):
-                cr, ci = coef_ref[b, 0, mode], coef_ref[b, 1, mode]
+                cr, ci = coef(mode)
                 ur, ui = probe_ref[mode, rows], probe_ref[mode, lower]
                 pr = pr + cr * ur - ci * ui
                 pi = pi + cr * ui + ci * ur
@@ -213,7 +247,7 @@
             lower = pl.ds(pl.multiple_of(base + length, BLOCK), BLOCK)
             real, imag = out_ref[rows], out_ref[lower]
             power = jnp.maximum(real * real + imag * imag, MAGNITUDE_FLOOR * MAGNITUDE_FLOOR)
-            factor = jnp.sqrt(inten_ref[b, rows] / power)
+            factor = jnp.sqrt(inten_ref[b_all, rows] / power)
             put_flat(rows, real * factor, imag * factor)
             return carry
 
@@ -244,11 +278,11 @@
                 terms_ref[part, spot, :] += placed.reshape(BLOCK + 8, columns)
             gr = wr * dr + wi * di
             gi = wr * di - wi * dr
-            for mode in range(modes):
-                cr, ci = coef_ref[b, 0, mode], coef_ref[b, 1, mode]
+            cr, ci = coef(me)
+            grad_ref[0, rows] += cr * gr + ci * gi
+            grad_ref[1, rows] += cr * gi - ci * gr
+            for mode in range(modes if own else 0):
                 ur, ui = probe_ref[mode, rows], probe_ref[mode, lower]
-                grad_ref[0, mode, rows] += cr * gr + ci * gi
-                grad_ref[1, mode, rows] += cr * gi - ci * gr
                 inner_ref[mode, 0] += folded(ur * gr + ui * gi)
                 inner_ref[mode, 1] += folded(ur * gi - ui * gr)
             return carry
@@ -259,28 +293,32 @@
             return jnp.sum(jnp.sum(value, axis=1, keepdims=True), axis=0, keepdims=True)
 
         weight = total(weight_ref[...]) * (1.0 / (length * length))
+        cr, ci = coef(me)
+        share = jnp.broadcast_to((cr * cr + ci * ci) * weight, (1, length))
+        for part in range(2):
+            grad_ref[part, length:] += jnp.broadcast_to(share, (EXTRA, length))
+        if not own:
+            return carry
         lanes = lax.broadcasted_iota(jnp.int32, (1, modes), 1)
         found = [jnp.zeros((1, modes), jnp.float32)] * 2
         for mode in range(modes):
-            cr, ci = coef_ref[b, 0, mode], coef_ref[b, 1, mode]
+            cr, ci = coef(mode)
             denominator = total(norm_ref[mode]) * weight + EPSILON
             for part, c in enumerate((cr, ci)):
                 value = c + total(inner_ref[mode, part]) / denominator
                 found[part] = jnp.where(lanes == mode, value, found[part])
-            share = jnp.broadcast_to((cr * cr + ci * ci) * weight, (1, length))
-            for part in range(2):
-                grad_ref[part, mode, length:] += jnp.broadcast_to(share, (EXTRA, length))
         coef_out_ref[b] = jnp.concatenate(found, axis=0)
         return carry
 
-    lax.fori_loop(0, count, pattern, 0)
-
-
-def reduce_kernel(scans, modes, terms_ref, grad_ref, object_ref, probe_ref,
+    lax.fori_loop(0, count, functools.partial(pattern, True), 0)
+    lax.fori_loop(count, patterns, functools.partial(pattern, False), 0)
+
+
+def reduce_kernel(scans, terms_ref, grad_ref, object_ref, probe_ref,
                   object_out_ref, probe_out_ref,
-                  core_in, mode_in, stage1, in1, stage2, in2, shift_in, stage_n, numer_in,
+                  core_in, stage1, in1, stage2, in2, shift_in,
                   send_g, recv_g, send_1, recv_1, send_2, recv_2, send_b, recv_b,
-                  send_s, recv_s, send_n, recv_n, send_a, recv_a):
+                  send_s, recv_s):
     s = lax.axis_index("scan")
     m = lax.axis_index("mode")
     r1, r2 = radices(scans)
@@ -289,7 +327,6 @@
     d1 = lax.rem(s // 2, r1)
     d2 = s // (2 * r1)
     b1, b2 = length // r1, length // (r1 * r2)
-    rows_m = length // modes
     sibling = (s + 1 - 2 * d0, m)
 
     def peer1(step):
@@ -298,11 +335,7 @@
     def peer2(step):
         return ((lax.rem(d2 + step, r2) * r1 + d1) * 2 + d0, m)
 
-    def peer_m(step):
-        return (s, lax.rem(m + step, modes))
-
     peers = [sibling] + [peer1(i) for i in range(1, r1)] + [peer2(i) for i in range(1, r2)]
-    peers += [peer_m(i) for i in range(1, modes)]
     barrier = pltpu.get_barrier_semaphore()
     for peer in peers:
         pl.semaphore_signal(barrier, inc=1, device_id=peer, device_id_type=MESH)
@@ -323,56 +356,24 @@
             src_ref=src, dst_ref=dst, send_sem=send, recv_sem=recv,
             device_id=peer, device_id_type=MESH)
 
-    def chunk(owner):
-        return pl.ds(pl.multiple_of(owner * rows_m, rows_m), rows_m)
-
-    def shift_copy(step, target):
-        owner = lax.rem(m + step, modes)
-        away = pl.ds(pl.multiple_of(length + owner * rows_m, rows_m), rows_m)
-        return remote(terms_ref.at[:, away], shift_in.at[:, chunk(owner)],
-                      send_s.at[step - 1], recv_s.at[step - 1], (target, m))
+    def shift_copy(target):
+        return remote(terms_ref.at[:, pl.ds(length, length)], shift_in, send_s, recv_s, (target, m))
 
     sends = []
-    core_copy = remote(grad_ref.at[1 - d0], core_in, send_g.at[0], recv_g.at[0], sibling)
+    core_copy = remote(grad_ref.at[1 - d0], core_in, send_g, recv_g, sibling)
     core_copy.start()
     sends.append(core_copy)
 
     @pl.when(s < scans - 1)
     def _():
-        for step in range(1, modes + 1):
-            shift_copy(step, s + 1).start()
+        shift_copy(s + 1).start()
 
     @pl.when(s == 0)
     def _():
         shift_in[...] = jnp.zeros_like(shift_in)
 
-    def shift_wait(step):
-        @pl.when(s > 0)
-        def _():
-            shift_copy(step, s - 1).wait_recv()
-
     core_copy.wait_recv()
-    mode_copies = []
-    for step in range(1, modes):
-        owner = lax.rem(m + step, modes)
-        core_in[owner] = core_in[owner] + grad_ref[d0, owner]
-        copy = remote(core_in.at[owner], mode_in.at[step - 1],
-                      send_g.at[step], recv_g.at[step], peer_m(step))
-        copy.start()
-        mode_copies.append(copy)
-    numer_copies = []
-    for step in range(1, modes):
-        owner = lax.rem(m + step, modes)
-        shift_wait(step)
-        stage_n[step - 1] = terms_ref[:, chunk(owner)] + shift_in[:, chunk(owner)]
-        copy = remote(stage_n.at[step - 1], numer_in.at[step - 1],
-                      send_n.at[step - 1], recv_n.at[step - 1], peer_m(step))
-        copy.start()
-        numer_copies.append(copy)
-    total = core_in[m] + grad_ref[d0, m]
-    for step in range(1, modes):
-        mode_copies[step - 1].wait_recv()
-        total = total + mode_in[step - 1]
+    total = core_in[...] + grad_ref[d0]
     for index in range(r1):
         stage1[index, :b1] = total[index * b1:(index + 1) * b1]
         stage1[index, b1:] = total[length:]
@@ -410,26 +411,6 @@
                       send_b.at[step - 1], recv_b.at[step - 1], peer2(step))
         copy.start()
         back2.append(copy)
-    shift_wait(modes)
-    for step in range(1, modes):
-        numer_copies[step - 1].wait_recv()
-    mine = chunk(m)
-
-    def owned(part):
-        value = terms_ref[part, mine] + shift_in[part, mine]
-        for step in range(1, modes):
-            value = value + numer_in[step - 1, part]
-        return value
-
-    scale = owned(2) + OBJECT_REGULARIZER
-    for part in range(2):
-        object_out_ref[part, mine] = object_ref[part, mine] + owned(part) / scale
-    object_copies = []
-    for step in range(1, modes):
-        copy = remote(object_out_ref.at[:, mine], object_out_ref.at[:, mine],
-                      send_a.at[step - 1], recv_a.at[step - 1], peer_m(step))
-        copy.start()
-        object_copies.append(copy)
     for copy in back2:
         copy.wait_recv()
     back1 = []
@@ -445,24 +426,33 @@
     back0 = remote(probe_out_ref.at[block0], probe_out_ref.at[block0],
                    send_b.at[slot], recv_b.at[slot], sibling)
     back0.start()
+
+    @pl.when(s > 0)
+    def _():
+        shift_copy(s - 1).wait_recv()
+
+    def owned(part):
+        return terms_ref[part, :length] + shift_in[part]
+
+    scale = owned(2) + OBJECT_REGULARIZER
+    for part in range(2):
+        object_out_ref[part] = object_ref[part] + owned(part) / scale
     back0.wait_recv()
-    for copy in object_copies:
-        copy.wait_recv()
 
     @pl.when(s < scans - 1)
     def _():
-        for step in range(1, modes + 1):
-            shift_copy(step, s + 1).wait_send()
-
-    for copy in sends + mode_copies + numer_copies + copies1 + copies2 + back2 + back1:
+        shift_copy(s + 1).wait_send()
+
+    for copy in sends + copies1 + copies2 + back2 + back1:
         copy.wait_send()
-    for copy in object_copies + [back0]:
+    for copy in [back0]:
         copy.wait_send()
 
 
 def on_device(scans, modes, object_field, eigen_probes, coeffs, intensities, positions):
     length = eigen_probes.shape[2]
     columns = object_field.shape[2]
+    count = intensities.shape[0]
     f32 = jnp.float32
     vmem = pl.BlockSpec(memory_space=pltpu.VMEM)
     smem = pl.BlockSpec(memory_space=pltpu.SMEM)
@@ -471,27 +461,30 @@
     others = max(modes - 1, 1)
     r1, r2 = radices(scans)
     b1, b2 = length // r1, length // (r1 * r2)
-    gathered, following = pl.pallas_call(
+    place = jnp.pad(positions, ((0, 8 - count), (0, 126)))
+    coef = jnp.pad(coeffs.reshape(count, 2 * modes), ((0, 8 - count), (0, 128 - 2 * modes)))
+    gathered, following, inten_all, place_all, coef_all = pl.pallas_call(
         functools.partial(gather_kernel, scans, modes),
         out_shape=(
             jax.ShapeDtypeStruct((modes, 2 * length, length), f32),
             jax.ShapeDtypeStruct(object_field.shape, f32),
+            jax.ShapeDtypeStruct((modes * count, length, length), f32),
+            jax.ShapeDtypeStruct((modes, 8, 128), jnp.int32),
+            jax.ShapeDtypeStruct((modes, 8, 128), f32),
         ),
-        in_specs=[vmem] * 2,
-        out_specs=(vmem, vmem),
-        scratch_shapes=[dma((others,))] * 4 + [dma, dma],
+        in_specs=[vmem] * 5,
+        out_specs=(vmem,) * 5,
+        scratch_shapes=[dma((others,))] * 4 + [dma, dma, dma((others, 3)), dma((others, 3))],
         compiler_params=pltpu.CompilerParams(
             collective_id=0, has_side_effects=True, vmem_limit_bytes=VMEM_BYTES),
         name="gather_probes",
-    )(probe, object_field)
-    row_start = positions[:, 0] - lax.axis_index("scan") * length
-    place = jnp.stack([row_start, positions[:, 1]], axis=1)
+    )(probe, object_field, intensities, place, coef)
     tables = [jnp.asarray(table) for table in dft_tables(length)]
     terms, grads, coeffs_new = pl.pallas_call(
         functools.partial(compute_kernel, modes),
         out_shape=(
             jax.ShapeDtypeStruct((3, 2 * length, columns), f32),
-            jax.ShapeDtypeStruct((2, modes, length + EXTRA, length), f32),
+            jax.ShapeDtypeStruct((2, length + EXTRA, length), f32),
             jax.ShapeDtypeStruct(coeffs.shape, f32),
         ),
         in_specs=[smem, smem] + [vmem] * 8,
@@ -510,10 +503,9 @@
         ],
         compiler_params=pltpu.CompilerParams(vmem_limit_bytes=VMEM_BYTES),
         name="local_terms",
-    )(place, coeffs, gathered, object_field, following, intensities, *tables)
-    rows_m = length // modes
+    )(place_all, coef_all, gathered, object_field, following, inten_all, *tables)
     object_new, probes_new = pl.pallas_call(
-        functools.partial(reduce_kernel, scans, modes),
+        functools.partial(reduce_kernel, scans),
         out_shape=(
             jax.ShapeDtypeStruct(object_field.shape, f32),
             jax.ShapeDtypeStruct((2 * length, length), f32),
@@ -521,22 +513,17 @@
         in_specs=[vmem] * 4,
         out_specs=(vmem, vmem),
         scratch_shapes=[
-            pltpu.VMEM((modes, length + EXTRA, length), f32),
-            pltpu.VMEM((others, length + EXTRA, length), f32),
+            pltpu.VMEM((length + EXTRA, length), f32),
             pltpu.VMEM((r1, b1 + EXTRA, length), f32),
             pltpu.VMEM((max(r1 - 1, 1), b1 + EXTRA, length), f32),
             pltpu.VMEM((r2, b2 + EXTRA, length), f32),
             pltpu.VMEM((max(r2 - 1, 1), b2 + EXTRA, length), f32),
             pltpu.VMEM((3, length, columns), f32),
-            pltpu.VMEM((others, 3, rows_m, columns), f32),
-            pltpu.VMEM((others, 3, rows_m, columns), f32),
-            dma((modes,)), dma((modes,)),
+            dma, dma,
             dma((max(r1 - 1, 1),)), dma((max(r1 - 1, 1),)),
             dma((max(r2 - 1, 1),)), dma((max(r2 - 1, 1),)),
             dma((r1 + r2 - 1,)), dma((r1 + r2 - 1,)),
-            dma((modes,)), dma((modes,)),
-            dma((others,)), dma((others,)),
-            dma((others,)), dma((others,)),
+            dma, dma,
         ],
         compiler_params=pltpu.CompilerParams(
             collective_id=1, has_side_effects=True, vmem_limit_bytes=VMEM_BYTES),

time: 77.3 us -> 95.4 us (1.23); the launches traced: 77.1 us -> 93.9 us
  Pallas kernels: 71 us -> 86.7 us
  local copies, waits for them, and re-layouts: 3.93 us -> 6.57 us
  other arithmetic: 1.46 us -> 0 us
    pallas_call x1, Pallas kernels: 15.7 us -> 26 us  [on_device(): pl.pallas_call(functools.partial(compute_kernel, modes), out_shape=(jax.S...]
    pallas_call x1, Pallas kernels: 13.6 us -> 23.8 us  [on_device(): pl.pallas_call(functools.partial(gather_kernel, scans, modes), out_shape=...]
    pallas_call x1, Pallas kernels: 41.8 us -> 36.9 us  [on_device(): pl.pallas_call(functools.partial(reduce_kernel, scans), out_shape=(jax.Sh...]
    pad x0 -> x2, local copies, waits for them, and re-layouts: none -> 1.87 us  [the longest x1 1.27 us: on_device(): place = jnp.pad(positions, ((0, 8 - count), (0, 126)))]
where the time goes in v1:
time: 95.4 us; the launch traced here: 93.9 us
  Pallas kernels  86.7 us (91%)
  local copies, waits for them, and re-layouts  6.57 us (7%)
    pallas_call x1, Pallas kernels, on_device(): pl.pallas_call(functools.partial(reduce_kernel, scans), out_shape=(jax.Sh...  36.9 us
    pallas_call x1, Pallas kernels, on_device(): pl.pallas_call(functools.partial(compute_kernel, modes), out_shape=(jax.S...  26 us
    pallas_call x1, Pallas kernels, on_device(): pl.pallas_call(functools.partial(gather_kernel, scans, modes), out_shape=...  23.8 us
    unnamed x2, local copies, waits for them, and re-layouts  3.93 us

profile of v1, /device:TPU:0, one launch (start us, length us, event | category | flops | bytes accessed | tf_op | source)
XLA Modules:
  0.0 93.9 jit_solution(12866419035412561478)
XLA Ops:
  0.6 0.8 reshape.16
  1.4 0.6 pad.9.coef_ref
  2.0 1.3 %pad.8.place_ref = s32[8,128]{1,0:T(8,128)} pad(s32[2,2]{1,0:T(2,128)} %param.13, s32[]{:T(128)} %constant.10.clone.1), padding=0_6x0_126 | pad | bytes 4116 | tf_op jit(solution)/shard_map/jit(_pad)/pad | solution.py:464
  3.3 23.8 %gather_probes.1 = (f32[2,512,256]{2,1,0:T(8,128)}, f32[2,256,384]{2,1,0:T(8,128)}, f32[4,256,256]{2,1,0:T(8,128)}, s32[2,8,128]{2,1,0:T(8,128)}, f32[2,8,128]{2,1,0:T(8,128)}) custom-call(f32[512,256]{1,0:T(8,128)} %bitcast.2, f32[2,256,384]{2,1,0:T(8,128)} %object_ref.3, f32[2,256,256]{2,1,0:T(8,128)} %inten_ref.1, s32[8,128]{1,0:T(8,128)} %pad.8.place_ref, ...), custom_call_target="tpu_custom_call" | custom-call | tf_op jit(solution)/shard_map/gather_probes/pallas_call | solution.py:466
  27.1 26.0 %local_terms.1 = (f32[3,512,384]{2,1,0:T(8,128)}, f32[2,264,256]{2,1,0:T(8,128)}, f32[2,2,2]{2,1,0:T(2,128)}) custom-call(s32[2,8,128]{2,1,0:T(8,128)} %get-tuple-element.13.place_ref, f32[2,8,128]{2,1,0:T(8,128)} %get-tuple-element.14.coef_ref, f32[2,512,256]{2,1,0:T(8,128)} %get-tuple-element.15.probe_ref, f32[2,256,384]{2,1,0:T(8,128)} %object_ref.3, ...), custom_call_target="tpu_custom_call" | custom-call | tf_op jit(solution)/shard_map/local_terms/pallas_call | solution.py:483
  53.1 36.9 %reduce_terms.1 = (f32[2,256,384]{2,1,0:T(8,128)}, f32[512,256]{1,0:T(8,128)}) custom-call(f32[3,512,384]{2,1,0:T(8,128)} %get-tuple-element.18.terms_ref, f32[2,264,256]{2,1,0:T(8,128)} %get-tuple-element.19.grad_ref, f32[2,256,384]{2,1,0:T(8,128)} %object_ref.3, f32[512,256]{1,0:T(8,128)} %bitcast.3), custom_call_target="tpu_custom_call" | custom-call | tf_op jit(solution)/shard_map/reduce_terms/pallas_call | solution.py:507
  90.0 2.1 %copy.14 = f32[2,256,384]{2,1,0:T(8,128)} copy(f32[2,256,384]{2,1,0:T(8,128)} %get-tuple-element.26) | data formatting | bytes 1572864
  92.0 1.9 %copy.15 = f32[1,2,256,256]{3,2,1,0:T(8,128)} copy(f32[1,2,256,256]{3,2,1,0:T(8,128)} %bitcast.4) | data formatting | bytes 1048576

commit v2 on v0

--- a/solution.py
+++ b/solution.py
@@ -14,7 +14,7 @@
 OBJECT_REGULARIZER = 1.0
 EPSILON = 1e-05
 MESH = pl.DeviceIdType.MESH
-BLOCK = 32
+BLOCK = 64
 EXTRA = 8
 VMEM_BYTES = 56 * 1024 * 1024
 
@@ -139,18 +139,26 @@
         return jnp.dot(a, b, preferred_element_type=jnp.float32)
 
     def right_apply(high_ref, low_ref):
-        high = flat_ref[:, :2 * length]
-        low = flat_ref[:, 2 * length:]
-        result = dot(high, high_ref[...]) + dot(low, high_ref[...]) + dot(high, low_ref[...])
-        for slot in range(2):
-            part_high, part_low = split(result[:, slot * length:(slot + 1) * length])
-            tall_ref[slot * length:(slot + 1) * length] = part_high
-            tall_ref[(2 + slot) * length:(3 + slot) * length] = part_low
+        size = length // 2
+        for start in range(0, length, size):
+            rows = slice(start, start + size)
+            for slot in range(2):
+                cols = slice(slot * length, (slot + 1) * length)
+                part = dot(
+                    jnp.concatenate([flat_ref[rows, :], flat_ref[rows, :2 * length]], axis=1),
+                    jnp.concatenate([high_ref[:, cols], high_ref[:, cols], low_ref[:, cols]], axis=0))
+                part_high, part_low = split(part)
+                base = slot * length + start
+                tall_ref[base:base + size] = part_high
+                tall_ref[base + 2 * length:base + 2 * length + size] = part_low
 
     def left_apply(high_ref, low_ref):
-        high = tall_ref[:2 * length]
-        low = tall_ref[2 * length:]
-        out_ref[...] = dot(high_ref[...], high) + dot(high_ref[...], low) + dot(low_ref[...], high)
+        size = length // 2
+        for start in range(0, 2 * length, size):
+            rows = slice(start, start + size)
+            out_ref[rows] = dot(
+                jnp.concatenate([high_ref[rows], high_ref[rows], low_ref[rows]], axis=1),
+                jnp.concatenate([tall_ref[...], tall_ref[:2 * length]], axis=0))
 
     norm_ref[...] = jnp.zeros_like(norm_ref)
 
@@ -247,8 +255,9 @@
             for mode in range(modes):
                 cr, ci = coef_ref[b, 0, mode], coef_ref[b, 1, mode]
                 ur, ui = probe_ref[mode, rows], probe_ref[mode, lower]
-                grad_ref[0, mode, rows] += cr * gr + ci * gi
-                grad_ref[1, mode, rows] += cr * gi - ci * gr
+                shifted = pl.ds(pl.multiple_of(base + EXTRA, 8), BLOCK)
+                grad_ref[0, mode, shifted] += cr * gr + ci * gi
+                grad_ref[1, mode, shifted] += cr * gi - ci * gr
                 inner_ref[mode, 0] += folded(ur * gr + ui * gi)
                 inner_ref[mode, 1] += folded(ur * gi - ui * gr)
             return carry
@@ -269,7 +278,7 @@
                 found[part] = jnp.where(lanes == mode, value, found[part])
             share = jnp.broadcast_to((cr * cr + ci * ci) * weight, (1, length))
             for part in range(2):
-                grad_ref[part, mode, length:] += jnp.broadcast_to(share, (EXTRA, length))
+                grad_ref[part, mode, :EXTRA] += jnp.broadcast_to(share, (EXTRA, length))
         coef_out_ref[b] = jnp.concatenate(found, axis=0)
         return carry
 
@@ -278,8 +287,9 @@
 
 def reduce_kernel(scans, modes, terms_ref, grad_ref, object_ref, probe_ref,
                   object_out_ref, probe_out_ref,
-                  core_in, mode_in, stage1, in1, stage2, in2, shift_in, stage_n, numer_in,
-                  send_g, recv_g, send_1, recv_1, send_2, recv_2, send_b, recv_b,
+                  core_in, mode_in, stage1, in1, stage2, in2, weight_ref, shift_in, stage_n, numer_in,
+                  send_g, recv_g, send_y, recv_y, send_1, recv_1, send_2, recv_2,
+                  back_s0, back_r0, back_s1, back_r1, back_s2, back_r2,
                   send_s, recv_s, send_n, recv_n, send_a, recv_a):
     s = lax.axis_index("scan")
     m = lax.axis_index("mode")
@@ -288,7 +298,6 @@
     d0 = lax.rem(s, 2)
     d1 = lax.rem(s // 2, r1)
     d2 = s // (2 * r1)
-    b1, b2 = length // r1, length // (r1 * r2)
     rows_m = length // modes
     sibling = (s + 1 - 2 * d0, m)
 
@@ -323,140 +332,168 @@
             src_ref=src, dst_ref=dst, send_sem=send, recv_sem=recv,
             device_id=peer, device_id_type=MESH)
 
-    def chunk(owner):
-        return pl.ds(pl.multiple_of(owner * rows_m, rows_m), rows_m)
-
-    def shift_copy(step, target):
-        owner = lax.rem(m + step, modes)
-        away = pl.ds(pl.multiple_of(length + owner * rows_m, rows_m), rows_m)
-        return remote(terms_ref.at[:, away], shift_in.at[:, chunk(owner)],
-                      send_s.at[step - 1], recv_s.at[step - 1], (target, m))
-
-    sends = []
-    core_copy = remote(grad_ref.at[1 - d0], core_in, send_g.at[0], recv_g.at[0], sibling)
-    core_copy.start()
-    sends.append(core_copy)
-
-    @pl.when(s < scans - 1)
-    def _():
-        for step in range(1, modes + 1):
-            shift_copy(step, s + 1).start()
-
-    @pl.when(s == 0)
-    def _():
-        shift_in[...] = jnp.zeros_like(shift_in)
-
-    def shift_wait(step):
+    parts = send_s.shape[1]
+    rows_c = rows_m // parts
+    pending = []
+
+    def begin(*arguments):
+        copy = remote(*arguments)
+        copy.start()
+        pending.append(copy)
+        return copy
+
+    def chunk(owner, part):
+        return pl.ds(pl.multiple_of(owner * rows_m + part * rows_c, rows_c), rows_c)
+
+    def shift_copy(step, part, target):
+        rows = chunk(lax.rem(m + step, modes), part)
+        away = chunk(lax.rem(m + step, modes) + modes, part)
+        return remote(terms_ref.at[:, away], shift_in.at[:, rows],
+                      send_s.at[step - 1, part], recv_s.at[step - 1, part], (target, m))
+
+    def shift_start(steps):
+        @pl.when(s < scans - 1)
+        def _():
+            for step in steps:
+                for part in range(parts):
+                    shift_copy(step, part, s + 1).start()
+
+    def shift_wait(step, part):
         @pl.when(s > 0)
         def _():
-            shift_copy(step, s - 1).wait_recv()
-
-    core_copy.wait_recv()
-    mode_copies = []
-    for step in range(1, modes):
-        owner = lax.rem(m + step, modes)
-        core_in[owner] = core_in[owner] + grad_ref[d0, owner]
-        copy = remote(core_in.at[owner], mode_in.at[step - 1],
-                      send_g.at[step], recv_g.at[step], peer_m(step))
-        copy.start()
-        mode_copies.append(copy)
-    numer_copies = []
-    for step in range(1, modes):
-        owner = lax.rem(m + step, modes)
-        shift_wait(step)
-        stage_n[step - 1] = terms_ref[:, chunk(owner)] + shift_in[:, chunk(owner)]
-        copy = remote(stage_n.at[step - 1], numer_in.at[step - 1],
-                      send_n.at[step - 1], recv_n.at[step - 1], peer_m(step))
-        copy.start()
-        numer_copies.append(copy)
-    total = core_in[m] + grad_ref[d0, m]
-    for step in range(1, modes):
-        mode_copies[step - 1].wait_recv()
-        total = total + mode_in[step - 1]
-    for index in range(r1):
-        stage1[index, :b1] = total[index * b1:(index + 1) * b1]
-        stage1[index, b1:] = total[length:]
-    copies1 = []
-    for step in range(1, r1):
-        copy = remote(stage1.at[lax.rem(d1 + step, r1)], in1.at[step - 1],
-                      send_1.at[step - 1], recv_1.at[step - 1], peer1(step))
-        copy.start()
-        copies1.append(copy)
-    total = stage1[d1]
-    for step in range(1, r1):
-        copies1[step - 1].wait_recv()
-        total = total + in1[step - 1]
-    for index in range(r2):
-        stage2[index, :b2] = total[index * b2:(index + 1) * b2]
-        stage2[index, b2:] = total[b1:]
-    copies2 = []
-    for step in range(1, r2):
-        copy = remote(stage2.at[lax.rem(d2 + step, r2)], in2.at[step - 1],
-                      send_2.at[step - 1], recv_2.at[step - 1], peer2(step))
-        copy.start()
-        copies2.append(copy)
-    total = stage2[d2]
-    for step in range(1, r2):
-        copies2[step - 1].wait_recv()
-        total = total + in2[step - 1]
-    block0 = pl.ds(pl.multiple_of(d0 * length, length), length)
-    start1 = d0 * length + d1 * b1
-    block1 = pl.ds(pl.multiple_of(start1, b1), b1)
-    block2 = pl.ds(pl.multiple_of(start1 + d2 * b2, b2), b2)
-    probe_out_ref[block2] = probe_ref[block2] + total[:b2] / total[b2:b2 + 1]
-    back2 = []
-    for step in range(1, r2):
-        copy = remote(probe_out_ref.at[block2], probe_out_ref.at[block2],
-                      send_b.at[step - 1], recv_b.at[step - 1], peer2(step))
-        copy.start()
-        back2.append(copy)
-    shift_wait(modes)
-    for step in range(1, modes):
-        numer_copies[step - 1].wait_recv()
-    mine = chunk(m)
-
-    def owned(part):
-        value = terms_ref[part, mine] + shift_in[part, mine]
+            shift_copy(step, part, s - 1).wait_recv()
+
+    def gradient(q):
+        size = length // groups
+        extra = EXTRA if q == 0 else 0
+        rows = pl.ds(0 if q == 0 else EXTRA + q * size, size + extra)
+        c1, c2 = size // r1, size // (r1 * r2)
+        core = begin(grad_ref.at[1 - d0, :, rows], core_in.at[:, rows],
+                     send_g.at[q], recv_g.at[q], sibling)
+        yield
+        core.wait_recv()
+        copies = []
         for step in range(1, modes):
-            value = value + numer_in[step - 1, part]
-        return value
-
-    scale = owned(2) + OBJECT_REGULARIZER
-    for part in range(2):
-        object_out_ref[part, mine] = object_ref[part, mine] + owned(part) / scale
-    object_copies = []
-    for step in range(1, modes):
-        copy = remote(object_out_ref.at[:, mine], object_out_ref.at[:, mine],
-                      send_a.at[step - 1], recv_a.at[step - 1], peer_m(step))
-        copy.start()
-        object_copies.append(copy)
-    for copy in back2:
-        copy.wait_recv()
-    back1 = []
-    for step in range(1, r1):
-        slot = r2 - 1 + step - 1
-        copy = remote(probe_out_ref.at[block1], probe_out_ref.at[block1],
-                      send_b.at[slot], recv_b.at[slot], peer1(step))
-        copy.start()
-        back1.append(copy)
-    for copy in back1:
-        copy.wait_recv()
-    slot = r2 + r1 - 2
-    back0 = remote(probe_out_ref.at[block0], probe_out_ref.at[block0],
-                   send_b.at[slot], recv_b.at[slot], sibling)
-    back0.start()
-    back0.wait_recv()
-    for copy in object_copies:
-        copy.wait_recv()
+            owner = lax.rem(m + step, modes)
+            core_in[owner, rows] = core_in[owner, rows] + grad_ref[d0, owner, rows]
+            copies.append(begin(core_in.at[owner, rows], mode_in.at[step - 1, rows],
+                                send_y.at[q, step - 1], recv_y.at[q, step - 1], peer_m(step)))
+        yield
+        total = core_in[m, rows] + grad_ref[d0, m, rows]
+        for step in range(1, modes):
+            copies[step - 1].wait_recv()
+            total = total + mode_in[step - 1, rows]
+        levels = ((r1, c1, d1, stage1, in1, send_1, recv_1, peer1),
+                  (r2, c2, d2, stage2, in2, send_2, recv_2, peer2))
+        for radix, c, digit, stage, landed, send, recv, peer in levels:
+            for index in range(radix):
+                if extra:
+                    stage[q, index, :extra] = total[:extra]
+                stage[q, index, extra:extra + c] = total[extra + index * c:extra + (index + 1) * c]
+            held = pl.ds(0, c + extra)
+            copies = []
+            for step in range(1, radix):
+                copies.append(begin(stage.at[q, lax.rem(digit + step, radix), held],
+                                    landed.at[q, step - 1, held],
+                                    send.at[q, step - 1], recv.at[q, step - 1], peer(step)))
+            yield
+            total = stage[q, digit, held]
+            for step in range(1, radix):
+                copies[step - 1].wait_recv()
+                total = total + landed[q, step - 1, held]
+        if extra:
+            weight_ref[...] = total[:extra]
+        start0 = d0 * length + q * size
+        start1 = start0 + d1 * c1
+        start2 = start1 + d2 * c2
+        block0 = pl.ds(pl.multiple_of(start0, size), size)
+        block1 = pl.ds(pl.multiple_of(start1, c1), c1)
+        block2 = pl.ds(pl.multiple_of(start2, c2), c2)
+        probe_out_ref[block2] = probe_ref[block2] + total[extra:] / weight_ref[0:1]
+        for block, radix, send, recv, peer in ((block2, r2, back_s2, back_r2, peer2),
+                                               (block1, r1, back_s1, back_r1, peer1),
+                                               (block0, 2, back_s0, back_r0, lambda step: sibling)):
+            copies = []
+            for step in range(1, radix):
+                copies.append(begin(probe_out_ref.at[block], probe_out_ref.at[block],
+                                    send.at[q, step - 1], recv.at[q, step - 1], peer(step)))
+            yield
+            for copy in copies:
+                copy.wait_recv()
+        yield
+
+    def terms():
+        copies = {}
+        for part in range(parts):
+            for step in range(1, modes):
+                rows = chunk(lax.rem(m + step, modes), part)
+                shift_wait(step, part)
+                stage_n[step - 1, part] = terms_ref[:, rows] + shift_in[:, rows]
+                copies[step, part] = begin(
+                    stage_n.at[step - 1, part], numer_in.at[step - 1, part],
+                    send_n.at[step - 1, part], recv_n.at[step - 1, part], peer_m(step))
+            if part == parts - 1:
+                shift_start([modes])
+            yield
+        back = []
+        for part in range(parts):
+            rows = chunk(m, part)
+            shift_wait(modes, part)
+            found = [terms_ref[k, rows] + shift_in[k, rows] for k in range(3)]
+            for step in range(1, modes):
+                copies[step, part].wait_recv()
+                found = [found[k] + numer_in[step - 1, part, k] for k in range(3)]
+            scale = found[2] + OBJECT_REGULARIZER
+            for k in range(2):
+                object_out_ref[k, rows] = object_ref[k, rows] + found[k] / scale
+            for step in range(1, modes):
+                back.append(begin(object_out_ref.at[:, rows], object_out_ref.at[:, rows],
+                                  send_a.at[step - 1, part], recv_a.at[step - 1, part], peer_m(step)))
+            yield
+        for copy in back:
+            copy.wait_recv()
+        yield
+
+    groups = send_g.shape[0]
+    chains = [gradient(q) for q in range(groups)]
+    objects = terms()
+
+    def advance():
+        for chain in chains:
+            next(chain)
+
+    advance()
+    shift_start(range(1, modes))
+
+    @pl.when(s == 0)
+    def _():
+        shift_in[...] = jnp.zeros_like(shift_in)
+
+    advance()
+    next(objects)
+    next(chains[0])
+    for _ in range(parts - 1):
+        next(objects)
+    for chain in chains[1:]:
+        next(chain)
+    advance()
+    for index in range(parts):
+        next(objects)
+        if index < 2:
+            advance()
+    for _ in range(2 - min(parts, 2)):
+        advance()
+    advance()
+    advance()
+    next(objects)
 
     @pl.when(s < scans - 1)
     def _():
         for step in range(1, modes + 1):
-            shift_copy(step, s + 1).wait_send()
-
-    for copy in sends + mode_copies + numer_copies + copies1 + copies2 + back2 + back1:
-        copy.wait_send()
-    for copy in object_copies + [back0]:
+            for part in range(parts):
+                shift_copy(step, part, s + 1).wait_send()
+
+    for copy in pending:
         copy.wait_send()
 
 
@@ -470,7 +507,10 @@
     probe = eigen_probes.reshape(2 * length, length)
     others = max(modes - 1, 1)
     r1, r2 = radices(scans)
-    b1, b2 = length // r1, length // (r1 * r2)
+    groups = 2 if length // (r1 * r2) >= 16 else 1
+    b1, b2 = length // (r1 * groups), length // (r1 * r2 * groups)
+    parts = 2 if modes == 2 else 1
+    rows_c = length // (modes * parts)
     gathered, following = pl.pallas_call(
         functools.partial(gather_kernel, scans, modes),
         out_shape=(
@@ -511,7 +551,6 @@
         compiler_params=pltpu.CompilerParams(vmem_limit_bytes=VMEM_BYTES),
         name="local_terms",
     )(place, coeffs, gathered, object_field, following, intensities, *tables)
-    rows_m = length // modes
     object_new, probes_new = pl.pallas_call(
         functools.partial(reduce_kernel, scans, modes),
         out_shape=(
@@ -523,20 +562,24 @@
         scratch_shapes=[
             pltpu.VMEM((modes, length + EXTRA, length), f32),
             pltpu.VMEM((others, length + EXTRA, length), f32),
-            pltpu.VMEM((r1, b1 + EXTRA, length), f32),
-            pltpu.VMEM((max(r1 - 1, 1), b1 + EXTRA, length), f32),
-            pltpu.VMEM((r2, b2 + EXTRA, length), f32),
-            pltpu.VMEM((max(r2 - 1, 1), b2 + EXTRA, length), f32),
+            pltpu.VMEM((groups, r1, b1 + EXTRA, length), f32),
+            pltpu.VMEM((groups, max(r1 - 1, 1), b1 + EXTRA, length), f32),
+            pltpu.VMEM((groups, r2, b2 + EXTRA, length), f32),
+            pltpu.VMEM((groups, max(r2 - 1, 1), b2 + EXTRA, length), f32),
+            pltpu.VMEM((EXTRA, length), f32),
             pltpu.VMEM((3, length, columns), f32),
-            pltpu.VMEM((others, 3, rows_m, columns), f32),
-            pltpu.VMEM((others, 3, rows_m, columns), f32),
-            dma((modes,)), dma((modes,)),
-            dma((max(r1 - 1, 1),)), dma((max(r1 - 1, 1),)),
-            dma((max(r2 - 1, 1),)), dma((max(r2 - 1, 1),)),
-            dma((r1 + r2 - 1,)), dma((r1 + r2 - 1,)),
-            dma((modes,)), dma((modes,)),
-            dma((others,)), dma((others,)),
-            dma((others,)), dma((others,)),
+            pltpu.VMEM((others, parts, 3, rows_c, columns), f32),
+            pltpu.VMEM((others, parts, 3, rows_c, columns), f32),
+            dma((groups,)), dma((groups,)),
+            dma((groups, others)), dma((groups, others)),
+            dma((groups, max(r1 - 1, 1))), dma((groups, max(r1 - 1, 1))),
+            dma((groups, max(r2 - 1, 1))), dma((groups, max(r2 - 1, 1))),
+            dma((groups, 1)), dma((groups, 1)),
+            dma((groups, max(r1 - 1, 1))), dma((groups, max(r1 - 1, 1))),
+            dma((groups, max(r2 - 1, 1))), dma((groups, max(r2 - 1, 1))),
+            dma((modes, parts)), dma((modes, parts)),
+            dma((others, parts)), dma((others, parts)),
+            dma((others, parts)), dma((others, parts)),
         ],
         compiler_params=pltpu.CompilerParams(
             collective_id=1, has_side_effects=True, vmem_limit_bytes=VMEM_BYTES),

time: 77.3 us -> 72 us (0.931)
  Pallas kernels: 71 us -> 65.7 us
    pallas_call x1, Pallas kernels: 15.7 us -> 13 us  [on_device(): pl.pallas_call(functools.partial(compute_kernel, modes), out_shape=(jax.S...]
    pallas_call x1, Pallas kernels: 41.8 us -> 39.2 us  [on_device(): pl.pallas_call(functools.partial(reduce_kernel, scans, modes), out_shape=...]
where the time goes in v2:
time: 72 us; the launch traced here: 71.8 us
  Pallas kernels  65.7 us (91%)
  local copies, waits for them, and re-layouts  3.93 us (5%)
  other arithmetic  1.46 us (2%)
    pallas_call x1, Pallas kernels, on_device(): pl.pallas_call(functools.partial(reduce_kernel, scans, modes), out_shape=...  39.2 us
    pallas_call x1, Pallas kernels, on_device(): pl.pallas_call(functools.partial(gather_kernel, scans, modes), out_shape=...  13.6 us
    pallas_call x1, Pallas kernels, on_device(): pl.pallas_call(functools.partial(compute_kernel, modes), out_shape=(jax.S...  13 us
    unnamed x2, local copies, waits for them, and re-layouts  3.93 us

profile of v2, /device:TPU:0, one launch (start us, length us, event | category | flops | bytes accessed | tf_op | source)
XLA Modules:
  0.0 71.8 jit_solution(14189013747877770021)
XLA Ops:
  0.6 0.8 %slice_subtract_fusion = (s32[2,1]{1,0:T(2,128)S(1)}, s32[2,1]{1,0:T(2,128)S(1)}) fusion(s32[2,2]{1,0:T(2,128)} %param.13, s32[]{:T(128)S(6)} %mul.3), kind=kLoop, calls=%fused_computation.1 | loop fusion | flops 2 | bytes 36 | tf_op jit(solution)/shard_map/sub | solution.py:527
  1.5 0.6 pad_add_fusion.place_ref
  2.1 13.6 %gather_probes.1 = (f32[2,512,256]{2,1,0:T(8,128)}, f32[2,256,384]{2,1,0:T(8,128)}) custom-call(f32[512,256]{1,0:T(8,128)} %bitcast.2, f32[2,256,384]{2,1,0:T(8,128)} %object_ref.3), custom_call_target="tpu_custom_call" | custom-call | tf_op jit(solution)/shard_map/gather_probes/pallas_call | solution.py:514
  15.7 13.0 %local_terms.1 = (f32[3,512,384]{2,1,0:T(8,128)}, f32[2,2,264,256]{3,2,1,0:T(8,128)}, f32[2,2,2]{2,1,0:T(2,128)}) custom-call(s32[2,2]{1,0:T(2,128)} %pad_add_fusion.place_ref, f32[2,2,2]{2,1,0:T(2,128)} %coef_ref.1, f32[2,512,256]{2,1,0:T(8,128)} %get-tuple-element.10.probe_ref, f32[2,256,384]{2,1,0:T(8,128)} %object_ref.3, ...), custom_call_target="tpu_custom_call" | custom-call | tf_op jit(solution)/shard_map/local_terms/pallas_call | solution.py:530
  28.7 39.2 %reduce_terms.1 = (f32[2,256,384]{2,1,0:T(8,128)}, f32[512,256]{1,0:T(8,128)}) custom-call(f32[3,512,384]{2,1,0:T(8,128)} %get-tuple-element.12.terms_ref, f32[2,2,264,256]{3,2,1,0:T(8,128)} %get-tuple-element.13.grad_ref, f32[2,256,384]{2,1,0:T(8,128)} %object_ref.3, f32[512,256]{1,0:T(8,128)} %bitcast.3), custom_call_target="tpu_custom_call" | custom-call | tf_op jit(solution)/shard_map/reduce_terms/pallas_call | solution.py:554
  67.8 2.1 %copy.14 = f32[2,256,384]{2,1,0:T(8,128)} copy(f32[2,256,384]{2,1,0:T(8,128)} %get-tuple-element.22) | data formatting | bytes 1572864
  69.9 1.9 %copy.15 = f32[1,2,256,256]{3,2,1,0:T(8,128)} copy(f32[1,2,256,256]{3,2,1,0:T(8,128)} %bitcast.4) | data formatting | bytes 1048576

commit v3 on v2

--- a/solution.py
+++ b/solution.py
@@ -85,12 +85,12 @@
             send_sem=send_c.at[step - 1], recv_sem=recv_c.at[step - 1],
             device_id=(sibling, m), device_id_type=MESH)
 
+    @pl.when(s > 0)
+    def _():
+        object_copy(s - 1).start()
+
     for step in range(1, modes):
         mode_copy(step).start()
-
-    @pl.when(s > 0)
-    def _():
-        object_copy(s - 1).start()
 
     gathered_ref[m] = probe_ref[...]
     for step in range(1, modes):
@@ -172,7 +172,7 @@
     lax.fori_loop(0, 2 * blocks, norms, 0)
 
     def pattern(b, carry):
-        top = place_ref[b, 0]
+        top = place_ref[b, 0] - lax.axis_index("scan") * length
         left = place_ref[b, 1]
         back_shift = lax.rem(columns - left, columns)
         within = lax.rem(top, 8)
@@ -285,7 +285,7 @@
     lax.fori_loop(0, count, pattern, 0)
 
 
-def reduce_kernel(scans, modes, terms_ref, grad_ref, object_ref, probe_ref,
+def reduce_kernel(scans, modes, terms_ref, grad_ref,
                   object_out_ref, probe_out_ref,
                   core_in, mode_in, stage1, in1, stage2, in2, weight_ref, shift_in, stage_n, numer_in,
                   send_g, recv_g, send_y, recv_y, send_1, recv_1, send_2, recv_2,
@@ -294,7 +294,7 @@
     s = lax.axis_index("scan")
     m = lax.axis_index("mode")
     r1, r2 = radices(scans)
-    length = object_ref.shape[1]
+    length = terms_ref.shape[1] // 2
     d0 = lax.rem(s, 2)
     d1 = lax.rem(s // 2, r1)
     d2 = s // (2 * r1)
@@ -409,7 +409,7 @@
         block0 = pl.ds(pl.multiple_of(start0, size), size)
         block1 = pl.ds(pl.multiple_of(start1, c1), c1)
         block2 = pl.ds(pl.multiple_of(start2, c2), c2)
-        probe_out_ref[block2] = probe_ref[block2] + total[extra:] / weight_ref[0:1]
+        probe_out_ref[block2] = total[extra:] / weight_ref[0:1]
         for block, radix, send, recv, peer in ((block2, r2, back_s2, back_r2, peer2),
                                                (block1, r1, back_s1, back_r1, peer1),
                                                (block0, 2, back_s0, back_r0, lambda step: sibling)):
@@ -445,7 +445,7 @@
                 found = [found[k] + numer_in[step - 1, part, k] for k in range(3)]
             scale = found[2] + OBJECT_REGULARIZER
             for k in range(2):
-                object_out_ref[k, rows] = object_ref[k, rows] + found[k] / scale
+                object_out_ref[k, rows] = found[k] / scale
             for step in range(1, modes):
                 back.append(begin(object_out_ref.at[:, rows], object_out_ref.at[:, rows],
                                   send_a.at[step - 1, part], recv_a.at[step - 1, part], peer_m(step)))
@@ -524,8 +524,6 @@
             collective_id=0, has_side_effects=True, vmem_limit_bytes=VMEM_BYTES),
         name="gather_probes",
     )(probe, object_field)
-    row_start = positions[:, 0] - lax.axis_index("scan") * length
-    place = jnp.stack([row_start, positions[:, 1]], axis=1)
     tables = [jnp.asarray(table) for table in dft_tables(length)]
     terms, grads, coeffs_new = pl.pallas_call(
         functools.partial(compute_kernel, modes),
@@ -550,14 +548,14 @@
         ],
         compiler_params=pltpu.CompilerParams(vmem_limit_bytes=VMEM_BYTES),
         name="local_terms",
-    )(place, coeffs, gathered, object_field, following, intensities, *tables)
-    object_new, probes_new = pl.pallas_call(
+    )(positions, coeffs, gathered, object_field, following, intensities, *tables)
+    object_step, probe_step = pl.pallas_call(
         functools.partial(reduce_kernel, scans, modes),
         out_shape=(
             jax.ShapeDtypeStruct(object_field.shape, f32),
             jax.ShapeDtypeStruct((2 * length, length), f32),
         ),
-        in_specs=[vmem] * 4,
+        in_specs=[vmem] * 2,
         out_specs=(vmem, vmem),
         scratch_shapes=[
             pltpu.VMEM((modes, length + EXTRA, length), f32),
@@ -584,8 +582,9 @@
         compiler_params=pltpu.CompilerParams(
             collective_id=1, has_side_effects=True, vmem_limit_bytes=VMEM_BYTES),
         name="reduce_terms",
-    )(terms, grads, object_field, probe)
-    return object_new, probes_new.reshape(eigen_probes.shape), coeffs_new
+    )(terms, grads)
+    probes_new = eigen_probes + probe_step.reshape(eigen_probes.shape)
+    return object_field + object_step, probes_new, coeffs_new
 
 
 def solution(mesh):

time: 72 us -> 69.3 us (0.962)
  local copies, waits for them, and re-layouts: 3.93 us -> 0.01 us
  other arithmetic: 1.46 us -> 3.01 us
    unnamed x2 -> x6, local copies, waits for them, and re-layouts: 3.93 us -> 0.01 us
    add x0 -> x2, other arithmetic: none -> 3.01 us  [the longest x1 2.15 us: on_device(): return (object_field + object_step, probes_new, coeffs_new)]
    sub x1 -> x0, other arithmetic: 0.83 us -> none  [on_device(): row_start = positions[:, 0] - lax.axis_index('scan') * length]
where the time goes in v3:
time: 69.3 us; the launch traced here: 69.2 us
  Pallas kernels  65.5 us (95%)
  other arithmetic  3.01 us (4%)
    pallas_call x1, Pallas kernels, on_device(): pl.pallas_call(functools.partial(reduce_kernel, scans, modes), out_shape=...  38.9 us
    pallas_call x1, Pallas kernels, on_device(): pl.pallas_call(functools.partial(gather_kernel, scans, modes), out_shape=...  13.6 us
    pallas_call x1, Pallas kernels, on_device(): pl.pallas_call(functools.partial(compute_kernel, modes), out_shape=(jax.S...  13 us
    add x1, other arithmetic, on_device(): return (object_field + object_step, probes_new, coeffs_new)  2.15 us

profile of v3, /device:TPU:0, one launch (start us, length us, event | category | flops | bytes accessed | tf_op | source)
XLA Modules:
  0.0 69.2 jit_solution(16704116766295119907)
XLA Ops:
  0.6 13.6 %gather_probes.1 = (f32[2,512,256]{2,1,0:T(8,128)}, f32[2,256,384]{2,1,0:T(8,128)}) custom-call(f32[512,256]{1,0:T(8,128)} %bitcast.2, f32[2,256,384]{2,1,0:T(8,128)} %own_ref.1), custom_call_target="tpu_custom_call" | custom-call | tf_op jit(solution)/shard_map/gather_probes/pallas_call | solution.py:514
  14.2 13.0 %local_terms.1 = (f32[3,512,384]{2,1,0:T(8,128)}, f32[2,2,264,256]{3,2,1,0:T(8,128)}, f32[2,2,2]{2,1,0:T(2,128)}) custom-call(s32[2,2]{1,0:T(2,128)} %place_ref.1, f32[2,2,2]{2,1,0:T(2,128)} %coef_ref.1, f32[2,512,256]{2,1,0:T(8,128)} %get-tuple-element.10.probe_ref, f32[2,256,384]{2,1,0:T(8,128)} %own_ref.1, f32[2,256,384]{2,1,0:T(8,128)} %get-tuple-element.11.next_ref, ...), custom_call_target="tpu_custom_call" | custom-call | tf_op jit(solution)/shard_map/local_terms/pallas_call | solution.py:528
  27.2 0.0 copy-start
  27.2 0.0 copy-start.1
  27.2 38.9 %reduce_terms.1 = (f32[2,256,384]{2,1,0:T(8,128)}, f32[512,256]{1,0:T(8,128)}) custom-call(f32[3,512,384]{2,1,0:T(8,128)} %get-tuple-element.12.terms_ref, f32[2,2,264,256]{3,2,1,0:T(8,128)} %get-tuple-element.13.grad_ref), custom_call_target="tpu_custom_call" | custom-call | tf_op jit(solution)/shard_map/reduce_terms/pallas_call | solution.py:552
  66.1 0.0 copy-start.2
  66.2 0.0 copy-done
  66.2 2.1 %add.6 = f32[2,256,384]{2,1,0:T(8,128)} add(f32[2,256,384]{2,1,0:T(8,128)S(1)} %copy-done, f32[2,256,384]{2,1,0:T(8,128)} %get-tuple-element.14) | non-fusion elementwise | flops 196608 | bytes 2359296 | tf_op jit(solution)/shard_map/add | solution.py:587
  68.3 0.0 copy-done.1
  68.3 0.0 copy-done.2
  68.3 0.9 %add.7 = f32[1,2,256,256]{3,2,1,0:T(8,128)} add(f32[1,2,256,256]{3,2,1,0:T(8,128)S(1)} %copy-done.1, f32[1,2,256,256]{3,2,1,0:T(8,128)S(1)} %bitcast.3) | non-fusion elementwise | flops 131072 | bytes 1572864 | tf_op jit(solution)/shard_map/add | solution.py:586
Async XLA Ops:
  27.2 39.0 %copy-start = (f32[2,256,384]{2,1,0:T(8,128)S(1)}, f32[2,256,384]{2,1,0:T(8,128)}, u32[]{:S(2)}) copy-start(f32[2,256,384]{2,1,0:T(8,128)} %own_ref.1) | copy-start | bytes 2359300
  27.2 41.1 %copy-start.1 = (f32[1,2,256,256]{3,2,1,0:T(8,128)S(1)}, f32[1,2,256,256]{3,2,1,0:T(8,128)}, u32[]{:S(2)}) copy-start(f32[1,2,256,256]{3,2,1,0:T(8,128)} %param.10) | copy-start | bytes 1572868
  66.1 2.2 %copy-start.2 = (f32[512,256]{1,0:T(8,128)S(1)}, f32[512,256]{1,0:T(8,128)}, u32[]{:S(2)}) copy-start(f32[512,256]{1,0:T(8,128)} %get-tuple-element.15) | copy-start | bytes 1572868

commit v4 on v3

--- a/solution.py
+++ b/solution.py
@@ -509,7 +509,7 @@
     r1, r2 = radices(scans)
     groups = 2 if length // (r1 * r2) >= 16 else 1
     b1, b2 = length // (r1 * groups), length // (r1 * r2 * groups)
-    parts = 2 if modes == 2 else 1
+    parts = 4 if modes == 2 else 1
     rows_c = length // (modes * parts)
     gathered, following = pl.pallas_call(
         functools.partial(gather_kernel, scans, modes),

time: 69.3 us -> 70.4 us (1.016)
  Pallas kernels: 65.5 us -> 66.6 us
    pallas_call x1, Pallas kernels: 38.9 us -> 40 us  [on_device(): pl.pallas_call(functools.partial(reduce_kernel, scans, modes), out_shape=...]
where the time goes in v4:
time: 70.4 us; the launch traced here: 70.3 us
  Pallas kernels  66.6 us (95%)
  other arithmetic  3.01 us (4%)
    pallas_call x1, Pallas kernels, on_device(): pl.pallas_call(functools.partial(reduce_kernel, scans, modes), out_shape=...  40 us
    pallas_call x1, Pallas kernels, on_device(): pl.pallas_call(functools.partial(gather_kernel, scans, modes), out_shape=...  13.6 us
    pallas_call x1, Pallas kernels, on_device(): pl.pallas_call(functools.partial(compute_kernel, modes), out_shape=(jax.S...  13 us
    add x1, other arithmetic, on_device(): return (object_field + object_step, probes_new, coeffs_new)  2.15 us

profile of v4, /device:TPU:0, one launch (start us, length us, event | category | flops | bytes accessed | tf_op | source)
XLA Modules:
  0.0 70.3 jit_solution(5142402189209424244)
XLA Ops:
  0.6 13.6 %gather_probes.1 = (f32[2,512,256]{2,1,0:T(8,128)}, f32[2,256,384]{2,1,0:T(8,128)}) custom-call(f32[512,256]{1,0:T(8,128)} %bitcast.2, f32[2,256,384]{2,1,0:T(8,128)} %own_ref.1), custom_call_target="tpu_custom_call" | custom-call | tf_op jit(solution)/shard_map/gather_probes/pallas_call | solution.py:514
  14.2 13.0 %local_terms.1 = (f32[3,512,384]{2,1,0:T(8,128)}, f32[2,2,264,256]{3,2,1,0:T(8,128)}, f32[2,2,2]{2,1,0:T(2,128)}) custom-call(s32[2,2]{1,0:T(2,128)} %place_ref.1, f32[2,2,2]{2,1,0:T(2,128)} %coef_ref.1, f32[2,512,256]{2,1,0:T(8,128)} %get-tuple-element.10.probe_ref, f32[2,256,384]{2,1,0:T(8,128)} %own_ref.1, f32[2,256,384]{2,1,0:T(8,128)} %get-tuple-element.11.next_ref, ...), custom_call_target="tpu_custom_call" | custom-call | tf_op jit(solution)/shard_map/local_terms/pallas_call | solution.py:528
  27.2 0.0 copy-start
  27.2 0.0 copy-start.1
  27.2 40.0 %reduce_terms.1 = (f32[2,256,384]{2,1,0:T(8,128)}, f32[512,256]{1,0:T(8,128)}) custom-call(f32[3,512,384]{2,1,0:T(8,128)} %get-tuple-element.12.terms_ref, f32[2,2,264,256]{3,2,1,0:T(8,128)} %get-tuple-element.13.grad_ref), custom_call_target="tpu_custom_call" | custom-call | tf_op jit(solution)/shard_map/reduce_terms/pallas_call | solution.py:552
  67.2 0.0 copy-start.2
  67.3 0.0 copy-done
  67.3 2.1 %add.6 = f32[2,256,384]{2,1,0:T(8,128)} add(f32[2,256,384]{2,1,0:T(8,128)S(1)} %copy-done, f32[2,256,384]{2,1,0:T(8,128)} %get-tuple-element.14) | non-fusion elementwise | flops 196608 | bytes 2359296 | tf_op jit(solution)/shard_map/add | solution.py:587
  69.4 0.0 copy-done.1
  69.4 0.0 copy-done.2
  69.4 0.9 %add.7 = f32[1,2,256,256]{3,2,1,0:T(8,128)} add(f32[1,2,256,256]{3,2,1,0:T(8,128)S(1)} %copy-done.1, f32[1,2,256,256]{3,2,1,0:T(8,128)S(1)} %bitcast.3) | non-fusion elementwise | flops 131072 | bytes 1572864 | tf_op jit(solution)/shard_map/add | solution.py:586
Async XLA Ops:
  27.2 40.1 %copy-start = (f32[2,256,384]{2,1,0:T(8,128)S(1)}, f32[2,256,384]{2,1,0:T(8,128)}, u32[]{:S(2)}) copy-start(f32[2,256,384]{2,1,0:T(8,128)} %own_ref.1) | copy-start | bytes 2359300
  27.2 42.2 %copy-start.1 = (f32[1,2,256,256]{3,2,1,0:T(8,128)S(1)}, f32[1,2,256,256]{3,2,1,0:T(8,128)}, u32[]{:S(2)}) copy-start(f32[1,2,256,256]{3,2,1,0:T(8,128)} %param.10) | copy-start | bytes 1572868
  67.2 2.2 %copy-start.2 = (f32[512,256]{1,0:T(8,128)S(1)}, f32[512,256]{1,0:T(8,128)}, u32[]{:S(2)}) copy-start(f32[512,256]{1,0:T(8,128)} %get-tuple-element.15) | copy-start | bytes 1572868
